TPU v7x, 32 devices: a whole 2x2x4 slice. The times are simulated.
32 devices in a mesh: rows: 8 (over z, y), cols: 4 (over x, core).
Axes of the slice: x: 2, y: 2, z: 4, core: 2. Of those that a mesh axis runs over, the one named last changes fastest.
Arguments:
- tiles: bfloat16 [2, 8, 4, 128, 128, 128], P(None, 'rows', 'cols'), may hold values from -0.15625 to 0.15625
- tile_scales: float32 [2, 8, 4, 128], P(None, 'rows', 'cols'), may hold values from 0.5 to 4
- tile_rows: int32 [2, 8, 4, 128], P(None, 'rows', 'cols'), may hold values from 0 to 7
- tile_cols: int32 [2, 8, 4, 128], P(None, 'rows', 'cols'), may hold values from 0 to 1023
- tile_counts: int32 [2, 8, 4], P(None, 'rows', 'cols'), may hold values from 32 to 128, as said below
- labels: int32 [2, 8192], P(None, 'rows'), may hold values from 0 to 31
- learning_rate: float32 [2], replicated, may hold values from 4 to 16
- weights: float32 [32, 524288], P(None, ('cols', 'rows')), may hold values from -6 to 6
Outputs:
- trained: float32 [32, 524288], P(None, ('cols', 'rows'))
- losses: float32 [2, 8192], P(None, ('rows', 'cols'))
Inputs may be any that keep to these rules, and one draw needn't show every extreme that they name: Only the first tile_counts[s, r, c] slots of a block are live; in every step some block has all 128 slots live.
All inputs are finite; a program needn't handle non-finite values.
Results may differ from a plain program's by a relative error of at most 0.0021.
Values may be sent and summed in bfloat16 or wider, within the bound.
A program may use at most 128 MiB of HBM per device.

v0:
```python
import jax
import jax.numpy as jnp
from jax import lax
from jax.sharding import PartitionSpec as P


def classify(class_scores, step_labels):
    exp_logits = jnp.exp(class_scores)
    denominator = jnp.sum(exp_logits, axis=0)
    class_ids = jnp.arange(class_scores.shape[0], dtype=jnp.int32)
    onehot = (class_ids[:, None] == step_labels[None, :]).astype(jnp.float32)
    sample_loss = jnp.log(denominator) - jnp.sum(onehot * class_scores, axis=0)
    residual = (exp_logits / denominator - onehot).astype(jnp.bfloat16)
    return (sample_loss, residual)


def per_device(
    tiles, tile_scales, tile_rows, tile_cols, tile_counts, labels, learning_rate, weights
):
    classes = weights.shape[0]
    tile_size = tiles.shape[-1]
    slot_count = tiles.shape[3]
    step_count = tiles.shape[0]
    sample_count = labels.shape[1]
    row_blocks = sample_count // tile_size
    owned_size = sample_count // lax.axis_size("cols")
    owned_start = lax.axis_index("cols") * owned_size
    slot_ids = jnp.arange(slot_count, dtype=jnp.int32)
    block_ids = jnp.arange(row_blocks, dtype=jnp.int32)
    current = weights
    step_losses = []
    for step_index in range(step_count):
        wide_bf = lax.all_gather(current.astype(jnp.bfloat16), "rows", axis=1, tiled=True)
        wide_blocks = wide_bf.reshape(classes, -1, tile_size)
        tile_entries = tiles[step_index, 0, 0]
        row_ids = tile_rows[step_index, 0, 0]
        col_ids = tile_cols[step_index, 0, 0]
        factor = jnp.where(
            slot_ids < tile_counts[step_index, 0, 0], tile_scales[step_index, 0, 0], 0.0
        )
        selected_weights = jnp.take(wide_blocks, col_ids, axis=1)
        weighted_products = jnp.einsum(
            "zei,eui->ezu", selected_weights, tile_entries, preferred_element_type=jnp.float32
        )
        row_indicator = (row_ids[:, None] == block_ids[None, :]).astype(jnp.float32) * factor[
            :, None
        ]
        partial_value = jnp.einsum(
            "iu,idq->duq", row_indicator, weighted_products, precision=lax.Precision.HIGHEST
        ).reshape(classes, sample_count)
        step_labels = labels[step_index]
        owned_logits = lax.psum_scatter(partial_value, "cols", scatter_dimension=1, tiled=True)
        owned_labels = lax.dynamic_slice_in_dim(step_labels, owned_start, owned_size)
        owned_loss, owned_residual = classify(owned_logits, owned_labels)
        residual = lax.all_gather(owned_residual, "cols", axis=1, tiled=True)
        step_losses.append(owned_loss)
        picked_rows = jnp.take(residual.reshape(classes, row_blocks, tile_size), row_ids, axis=1)
        grad_blocks = (
            jnp.einsum(
                "cts,tsf->ctf", picked_rows, tile_entries, preferred_element_type=jnp.float32
            )
            * factor[None, :, None]
        )
        local_grad = (
            jnp.zeros((classes, wide_blocks.shape[1], tile_size), jnp.float32)
            .at[:, col_ids, :]
            .add(grad_blocks)
            .reshape(classes, -1)
        )
        step_rate = learning_rate[step_index]
        grad_share = lax.psum_scatter(local_grad, "rows", scatter_dimension=1, tiled=True)
        current = current - step_rate * grad_share
    return (current, jnp.stack(step_losses))


def solution(mesh):
    return jax.shard_map(
        per_device,
        mesh=mesh,
        in_specs=(
            P(None, "rows", "cols", None, None, None),
            P(None, "rows", "cols", None),
            P(None, "rows", "cols", None),
            P(None, "rows", "cols", None),
            P(None, "rows", "cols"),
            P(None, "rows"),
            P(),
            P(None, ("cols", "rows")),
        ),
        out_specs=(P(None, ("cols", "rows")), P(None, ("rows", "cols"))),
        check_vma=False,
    )
```

profile of v0, /device:TPU:13, one launch (start us, length us, event | category | flops | bytes accessed | tf_op | source)
XLA Modules:
  0.0 1003.9 jit_solution(15706906852062940685)
XLA Ops:
  7.3 2.7 convert_element_type.20
  10.7 1.3 compare_select_fusion.6
  12.0 121.1 %all-gather.3.cloned.1.call-done = bf16[32,131072]{1,0:T(8,128)(2,1)} async-done(((bf16[32,16384]{1,0:T(8,128)(2,1)}), bf16[32,131072]{1,0:T(8,128)(2,1)}) %all-gather.3.cloned.1.call-update) | async-done | bytes 8388624 | tf_op jit(solution)/shard_map/all_gather | solution.py:33
  133.1 8.0 copy_bitcast_fusion.3
  141.1 4.1 gather_fusion
  145.3 4.5 fusion.6
  149.8 2.4 fusion.14
  152.9 20.6 %reduce-scatter.5.cloned.1.call-done = f32[32,256]{1,0:T(8,128)} async-done(((f32[32,1024]{1,0:T(8,128)}), f32[32,256]{1,0:T(8,128)}) %reduce-scatter.5.cloned.1.call-update) | async-done | bytes 32784 | tf_op jit(solution)/shard_map/reduce_scatter | solution.py:52
  173.6 0.8 select_reduce_fusion.1
  174.4 0.8 subtract_convert_fusion.1
  175.2 6.3 all_gather.13
  182.2 3.5 fusion.16
  185.7 7.9 broadcast.87.clone
  193.5 15.5 %scatter_fusion = f32[32,1024,128]{2,0,1:T(8,128)} fusion(f32[32,1024,128]{2,0,1:T(8,128)} %broadcast.87.clone, s32[128]{0:T(128)S(1)} %get-tuple-element.26, f32[128,32,128]{2,1,0:T(8,128)S(1)} %fusion.16), kind=kCustom, calls=%fused_computation.4 | custom fusion | flops 524288 | bytes 6291968 | tf_op jit(solution)/shard_map/scatter-add | solution.py:67
  209.1 11.3 %copy_bitcast_fusion.1 = f32[32,131072]{1,0:T(8,128)} fusion(f32[32,1024,128]{2,0,1:T(8,128)} %scatter_fusion), kind=kLoop, calls=%fused_computation.7 | loop fusion | bytes 33554432 | tf_op jit(solution)/shard_map/reshape | solution.py:68
  221.7 276.6 %reduce-scatter.7.cloned.1.call-done = f32[32,16384]{1,0:T(8,128)} async-done(((f32[32,131072]{1,0:T(8,128)}), f32[32,16384]{1,0:T(8,128)}) %reduce-scatter.7.cloned.1.call-update) | async-done | bytes 2097168 | tf_op jit(solution)/shard_map/reduce_scatter | solution.py:71
  498.3 3.4 fusion.34
  502.0 121.6 %all-gather.5.cloned.1.call-done = bf16[32,131072]{1,0:T(8,128)(2,1)} async-done(((bf16[32,16384]{1,0:T(8,128)(2,1)}), bf16[32,131072]{1,0:T(8,128)(2,1)}) %all-gather.5.cloned.1.call-update) | async-done | bytes 8388624 | tf_op jit(solution)/shard_map/all_gather | solution.py:33
  623.6 8.0 copy_bitcast_fusion.2
  631.7 4.1 gather_fusion.2
  635.8 4.5 fusion.2
  640.3 2.4 fusion.12
  643.5 20.6 %reduce-scatter.9.cloned.1.call-done = f32[32,256]{1,0:T(8,128)} async-done(((f32[32,1024]{1,0:T(8,128)}), f32[32,256]{1,0:T(8,128)}) %reduce-scatter.9.cloned.1.call-update) | async-done | bytes 32784 | tf_op jit(solution)/shard_map/reduce_scatter | solution.py:52
  664.1 0.8 select_reduce_fusion
  664.9 0.8 subtract_convert_fusion
  665.7 6.3 all_gather.15
  672.7 4.8 fusion.19
  677.5 7.9 broadcast.87
  685.4 17.4 %scatter_fusion.1 = f32[32,1024,128]{2,0,1:T(8,128)} fusion(f32[32,1024,128]{2,0,1:T(8,128)} %broadcast.87, s32[128]{0:T(128)S(1)} %get-tuple-element.27, f32[128,32,128]{2,1,0:T(8,128)} %fusion.19), kind=kCustom, calls=%fused_computation.5 | custom fusion | flops 524288 | bytes 6291968 | tf_op jit(solution)/shard_map/scatter-add | solution.py:67
  702.8 11.3 %copy_bitcast_fusion = f32[32,131072]{1,0:T(8,128)} fusion(f32[32,1024,128]{2,0,1:T(8,128)} %scatter_fusion.1), kind=kLoop, calls=%fused_computation.6 | loop fusion | bytes 33554432 | tf_op jit(solution)/shard_map/reshape | solution.py:68
  714.8 277.2 %reduce-scatter.11.cloned.1.call-done = f32[32,16384]{1,0:T(8,128)} async-done(((f32[32,131072]{1,0:T(8,128)}), f32[32,16384]{1,0:T(8,128)}) %reduce-scatter.11.cloned.1.call-update) | async-done | bytes 2097168 | tf_op jit(solution)/shard_map/reduce_scatter | solution.py:71
  992.0 5.1 multiply_subtract_fusion
  (48 shorter events, 5.9 us)
Async XLA Ops:
  7.2 2.8 copy-start.3
  7.2 2.9 copy-start.2
  7.2 2.9 copy-start.4
  7.2 3.5 copy-start.6
  7.2 4.8 copy-start.1
  7.2 125.9 %all-gather.3.cloned.1.call-start = ((), (), s32[]{:S(2)}) async-start(), calls=%async_computation.4 | async-start | bytes 9437184 | tf_op jit(solution)/shard_map/all_gather | solution.py:33
  10.0 163.6 %reduce-scatter.5.cloned.1.call-start = ((), (), s32[]{:S(2)}) async-start(), calls=%async_computation.5 | async-start | bytes 163840 | tf_op jit(solution)/shard_map/reduce_scatter | solution.py:52
  152.9 345.4 %reduce-scatter.7.cloned.1.call-start = ((), (), s32[]{:S(2)}) async-start(), calls=%async_computation.6 | async-start | bytes 18874368 | tf_op jit(solution)/shard_map/reduce_scatter | solution.py:71
  220.4 0.7 copy-start.5
  220.4 277.9 %copy-start = (f32[32,16384]{1,0:T(8,128)S(1)}, f32[32,16384]{1,0:T(8,128)}, u32[]{:S(2)}) copy-start(f32[32,16384]{1,0:T(8,128)} %param.19) | copy-start | bytes 6291460
  220.4 403.2 %all-gather.5.cloned.1.call-start = ((), (), s32[]{:S(2)}) async-start(), calls=%async_computation.7 | async-start | bytes 9437184 | tf_op jit(solution)/shard_map/all_gather | solution.py:33
  501.8 162.3 %reduce-scatter.9.cloned.1.call-start = ((), (), s32[]{:S(2)}) async-start(), calls=%async_computation.8 | async-start | bytes 163840 | tf_op jit(solution)/shard_map/reduce_scatter | solution.py:52
  643.4 348.6 %reduce-scatter.11.cloned.1.call-start = ((), (), s32[]{:S(2)}) async-start(), calls=%async_computation.9 | async-start | bytes 18874368 | tf_op jit(solution)/shard_map/reduce_scatter | solution.py:71
Sparse Core Ops, SparseCore 0:
  10.8 122.2 all-gather.2
  153.0 20.5 reduce-scatter.4
  220.5 277.7 reduce-scatter.6
  501.9 121.6 all-gather.4
  643.5 20.5 reduce-scatter.8
  714.3 277.6 reduce-scatter.10
where the time goes:
time: 1010 us; the launch traced here: 1000 us
  waiting for transfers between devices  838 us (83%)
  local copies, waits for them, and re-layouts  67.5 us (7%)
  other arithmetic  49.2 us (5%)
  matrix products  22 us (2%)
  between operations  14.3 us (1%)
  blocking collectives  12.6 us (1%)
    reduce_scatter x2, waiting for transfers between devices, per_device(): lax.psum_scatter(local_grad, 'rows', scatter_dimension=1, tiled=True)  554 us
    all_gather x2, waiting for transfers between devices, per_device(): lax.all_gather(current.astype(jnp.bfloat16), 'rows', axis=1, tiled=True)  243 us
    reduce_scatter x2, waiting for transfers between devices, per_device(): lax.psum_scatter(partial_value, 'cols', scatter_dimension=1, tiled=True)  41.3 us
    scatter-add x2, other arithmetic, per_device(): local_grad = jnp.zeros((classes, wide_blocks.shape[1], tile_size), jnp.fl...  33 us
    reshape x2, local copies, waits for them, and re-layouts, per_device(): local_grad = jnp.zeros((classes, wide_blocks.shape[1], tile_size), jnp.fl...  22.6 us
  transfers between devices with their start and end apart: 6, of which 6 were waited for; matrix products, arithmetic and copies ran while one was open for 0% of the time, Pallas kernels for 0%

commit v1 on v0

--- a/solution.py
+++ b/solution.py
@@ -1,7 +1,14 @@
+import functools
+import math
 import jax
 import jax.numpy as jnp
 from jax import lax
+from jax.experimental import pallas as pl
+from jax.experimental.pallas import tpu as pltpu
 from jax.sharding import PartitionSpec as P
+
+MESH = pl.DeviceIdType.MESH
+VMEM_LIMIT = 48 * 1024 * 1024
 
 
 def classify(class_scores, step_labels):
@@ -14,7 +21,7 @@
     return (sample_loss, residual)
 
 
-def per_device(
+def dense_program(
     tiles, tile_scales, tile_rows, tile_cols, tile_counts, labels, learning_rate, weights
 ):
     classes = weights.shape[0]
@@ -73,6 +80,317 @@
     return (current, jnp.stack(step_losses))
 
 
+def lanes(block, size):
+    return pl.ds(pl.multiple_of(block * size, size), size)
+
+
+def pack_body(size, next_ref, weights_ref, send_ref):
+    @pl.loop(0, send_ref.shape[0] // 8)
+    def _(group):
+        for lane in range(8):
+            entry = group * 8 + lane
+            send_ref[entry] = weights_ref[:, lanes(next_ref[entry], size)].astype(jnp.bfloat16)
+
+
+def apply_body(size, here_ref, rate_ref, weights_ref, grads_ref, out_ref):
+    out_ref[...] = weights_ref[...]
+    rate = rate_ref[0]
+
+    @pl.loop(0, grads_ref.shape[0] // 8)
+    def _(group):
+        for lane in range(8):
+            entry = group * 8 + lane
+            where = lanes(here_ref[entry], size)
+            out_ref[:, where] -= rate * grads_ref[entry].astype(jnp.float32)
+
+
+def pack_kernel(size, next_ref, weights_ref, send_ref):
+    pack_body(size, next_ref, weights_ref, send_ref)
+
+
+def apply_kernel(size, here_ref, rate_ref, weights_ref, grads_ref, out_ref):
+    apply_body(size, here_ref, rate_ref, weights_ref, grads_ref, out_ref)
+
+
+def apply_pack_kernel(
+    size, here_ref, next_ref, rate_ref, weights_ref, grads_ref, out_ref, send_ref
+):
+    apply_body(size, here_ref, rate_ref, weights_ref, grads_ref, out_ref)
+    pack_body(size, next_ref, out_ref, send_ref)
+
+
+def exchange_kernel(axis, count, send_ref, recv_ref, send_sems, recv_sems, own_sem):
+    me = lax.axis_index(axis)
+    barrier = pltpu.get_barrier_semaphore()
+    for shift in range(1, count):
+        peer = lax.rem(me + shift, count)
+        pl.semaphore_signal(barrier, inc=1, device_id={axis: peer}, device_id_type=MESH)
+    own = pltpu.make_async_copy(send_ref.at[me], recv_ref.at[me], own_sem)
+    own.start()
+    pl.semaphore_wait(barrier, count - 1)
+    copies = []
+    for shift in range(1, count):
+        peer = lax.rem(me + shift, count)
+        copy = pltpu.make_async_remote_copy(
+            src_ref=send_ref.at[peer],
+            dst_ref=recv_ref.at[me],
+            send_sem=send_sems.at[shift],
+            recv_sem=recv_sems.at[shift],
+            device_id={axis: peer},
+            device_id_type=MESH,
+        )
+        copy.start()
+        copies.append(copy)
+    own.wait()
+    for copy in copies:
+        copy.wait()
+
+
+def exchange(send, axis, count, collective_id):
+    return pl.pallas_call(
+        functools.partial(exchange_kernel, axis, count),
+        out_shape=jax.ShapeDtypeStruct(send.shape, send.dtype),
+        in_specs=[pl.BlockSpec(memory_space=pl.ANY)],
+        out_specs=pl.BlockSpec(memory_space=pl.ANY),
+        scratch_shapes=[
+            pltpu.SemaphoreType.DMA((count,)),
+            pltpu.SemaphoreType.DMA((count,)),
+            pltpu.SemaphoreType.DMA,
+        ],
+        compiler_params=pltpu.CompilerParams(collective_id=collective_id, has_side_effects=True),
+        name="exchange",
+    )(send)
+
+
+def scores_kernel(group, size, place_ref, row_ref, factor_ref, recv_ref, tiles_ref, out_ref):
+    first = pl.program_id(0) * group
+
+    @pl.when(first == 0)
+    def _():
+        out_ref[...] = jnp.zeros_like(out_ref)
+
+    products = []
+    for slot in range(group):
+        product = lax.dot_general(
+            recv_ref[place_ref[first + slot]],
+            tiles_ref[0, 0, 0, slot],
+            (((1,), (1,)), ((), ())),
+            preferred_element_type=jnp.float32,
+        )
+        products.append(product * factor_ref[first + slot])
+    for slot in range(group):
+        out_ref[:, lanes(row_ref[first + slot], size)] += products[slot]
+
+
+def classify_kernel(
+    axis, count, part_ref, labels_ref, residual_ref, loss_ref, held, send_sems, recv_sems
+):
+    me = lax.axis_index(axis)
+    barrier = pltpu.get_barrier_semaphore()
+    for shift in range(1, count):
+        peer = lax.rem(me + shift, count)
+        pl.semaphore_signal(barrier, inc=1, device_id={axis: peer}, device_id_type=MESH)
+    pl.semaphore_wait(barrier, count - 1)
+    copies = []
+    for shift in range(1, count):
+        peer = lax.rem(me + shift, count)
+        copy = pltpu.make_async_remote_copy(
+            src_ref=part_ref,
+            dst_ref=held.at[shift],
+            send_sem=send_sems.at[shift],
+            recv_sem=recv_sems.at[shift],
+            device_id={axis: peer},
+            device_id_type=MESH,
+        )
+        copy.start()
+        copies.append(copy)
+    scores = part_ref[...]
+    for shift, copy in enumerate(copies):
+        copy.wait()
+        scores = scores + held[shift + 1]
+    exp_scores = jnp.exp(scores)
+    total = jnp.sum(exp_scores, axis=0, keepdims=True)
+    class_ids = lax.broadcasted_iota(jnp.int32, scores.shape, 0)
+    onehot = (class_ids == labels_ref[...]).astype(jnp.float32)
+    loss_ref[...] = jnp.log(total) - jnp.sum(onehot * scores, axis=0, keepdims=True)
+    residual_ref[...] = (exp_scores / total - onehot).astype(jnp.bfloat16)
+
+
+def grads_kernel(
+    group, size, place_ref, row_ref, factor_ref, residual_ref, tiles_ref, out_ref, total
+):
+    first = pl.program_id(0) * group
+
+    @pl.when(first == 0)
+    def _():
+        total[...] = jnp.zeros_like(total)
+
+    products = []
+    for slot in range(group):
+        product = jnp.dot(
+            residual_ref[:, lanes(row_ref[first + slot], size)],
+            tiles_ref[0, 0, 0, slot],
+            preferred_element_type=jnp.float32,
+        )
+        products.append(product * factor_ref[first + slot])
+    for slot in range(group):
+        total[place_ref[first + slot]] += products[slot]
+
+    @pl.when(pl.program_id(0) == pl.num_programs(0) - 1)
+    def _():
+        out_ref[...] = total[...].astype(jnp.bfloat16)
+
+
+VM = pl.BlockSpec(memory_space=pltpu.VMEM)
+SM = pl.BlockSpec(memory_space=pltpu.SMEM)
+LOCAL = pltpu.CompilerParams(vmem_limit_bytes=VMEM_LIMIT)
+
+
+def slot_call(kernel, step, tiles, scalars, operand, out_shape, scratch, name):
+    group = 16
+    size = tiles.shape[-1]
+    zeros = lambda rank: (lambda i, *_: (0,) * rank)
+    return pl.pallas_call(
+        functools.partial(kernel, group, size),
+        grid_spec=pltpu.PrefetchScalarGridSpec(
+            num_scalar_prefetch=3,
+            grid=(tiles.shape[3] // group,),
+            in_specs=[
+                pl.BlockSpec(operand.shape, zeros(operand.ndim)),
+                pl.BlockSpec((1, 1, 1, group, size, size), lambda i, *_: (step, 0, 0, i, 0, 0)),
+            ],
+            out_specs=pl.BlockSpec(out_shape.shape, zeros(len(out_shape.shape))),
+            scratch_shapes=scratch,
+        ),
+        out_shape=out_shape,
+        compiler_params=LOCAL,
+        name=name,
+    )(*scalars, operand, tiles)
+
+
+def sparse_program(
+    capacity, places, requests,
+    tiles, tile_scales, tile_rows, tile_cols, tile_counts, labels, learning_rate, weights
+):
+    classes = weights.shape[0]
+    size = tiles.shape[-1]
+    steps, slots = tiles.shape[0], tiles.shape[3]
+    n_rows, n_cols = lax.axis_size("rows"), lax.axis_size("cols")
+    samples = labels.shape[1]
+    entries = n_rows * capacity
+    packed = jax.ShapeDtypeStruct((entries, classes, size), jnp.bfloat16)
+    slot_ids = jnp.arange(slots, dtype=jnp.int32)
+    owned = samples // n_cols
+    trade = lambda x: exchange(
+        x.reshape(n_rows, capacity, classes, size), "rows", n_rows, 0
+    ).reshape(packed.shape)
+
+    current = weights
+    send = pl.pallas_call(
+        functools.partial(pack_kernel, size),
+        out_shape=packed, in_specs=[SM, VM], out_specs=VM, compiler_params=LOCAL, name="pack",
+    )(requests[0], current)
+    losses = []
+    for step in range(steps):
+        factor = jnp.where(slot_ids < tile_counts[step, 0, 0], tile_scales[step, 0, 0], 0.0)
+        scalars = (places[step], tile_rows[step, 0, 0], factor)
+        part = slot_call(
+            scores_kernel, step, tiles, scalars, trade(send),
+            jax.ShapeDtypeStruct((classes, samples), jnp.float32), [], "scores",
+        )
+        residual, loss = pl.pallas_call(
+            functools.partial(classify_kernel, "cols", n_cols),
+            out_shape=(
+                jax.ShapeDtypeStruct((classes, samples), jnp.bfloat16),
+                jax.ShapeDtypeStruct((1, samples), jnp.float32),
+            ),
+            in_specs=[VM, VM],
+            out_specs=(VM, VM),
+            scratch_shapes=[
+                pltpu.VMEM((n_cols, classes, samples), jnp.float32),
+                pltpu.SemaphoreType.DMA((n_cols,)),
+                pltpu.SemaphoreType.DMA((n_cols,)),
+            ],
+            compiler_params=pltpu.CompilerParams(collective_id=1, has_side_effects=True),
+            name="classify",
+        )(part, labels[step][None])
+        losses.append(lax.dynamic_slice_in_dim(loss[0], lax.axis_index("cols") * owned, owned))
+        grads = trade(
+            slot_call(
+                grads_kernel, step, tiles, scalars, residual, packed,
+                [pltpu.VMEM((entries, classes, size), jnp.float32)], "grads",
+            )
+        )
+        rate = lax.slice_in_dim(learning_rate, step, step + 1)
+        shape = jax.ShapeDtypeStruct(current.shape, current.dtype)
+        if step + 1 < steps:
+            current, send = pl.pallas_call(
+                functools.partial(apply_pack_kernel, size),
+                out_shape=(shape, packed), in_specs=[SM, SM, SM, VM, VM], out_specs=(VM, VM),
+                compiler_params=LOCAL, name="apply_pack",
+            )(requests[step], requests[step + 1], rate, current, grads)
+        else:
+            current = pl.pallas_call(
+                functools.partial(apply_kernel, size),
+                out_shape=shape, in_specs=[SM, SM, VM, VM], out_specs=VM,
+                compiler_params=LOCAL, name="apply",
+            )(requests[step], rate, current, grads)
+    return current, jnp.stack(losses)
+
+
+def per_device(
+    tiles, tile_scales, tile_rows, tile_cols, tile_counts, labels, learning_rate, weights
+):
+    args = (tiles, tile_scales, tile_rows, tile_cols, tile_counts, labels, learning_rate, weights)
+    size, slots = tiles.shape[-1], tiles.shape[3]
+    n_rows, n_cols = lax.axis_size("rows"), lax.axis_size("cols")
+    per_owner = weights.shape[1] // size
+    mean = slots / n_rows
+    capacity = min(per_owner, slots, 4 * math.ceil((mean + 3 * math.sqrt(mean)) / 4))
+    slot_ids = jnp.arange(slots, dtype=jnp.int32)
+
+    live = slot_ids < tile_counts[:, 0, 0, None]
+    mine = jnp.where(live, tile_cols[:, 0, 0], -1)
+    everyone = lax.all_gather(mine, ("rows", "cols"), axis=0)
+    owner = jnp.where(everyone >= 0, everyone // per_owner, -1)
+    same = everyone[..., :, None] == everyone[..., None, :]
+    before = slot_ids[:, None] > slot_ids[None, :]
+    fresh = (everyone >= 0) & ~jnp.any(same & before, axis=-1)
+    lower = (owner[..., :, None] == owner[..., None, :]) & (
+        everyone[..., None, :] < everyone[..., :, None]
+    )
+    rank = jnp.sum((lower & fresh[..., None, :]).astype(jnp.int32), axis=-1)
+    rank = jnp.where(everyone >= 0, rank, 0)
+    most = jnp.max(rank) + 1
+
+    row, col = lax.axis_index("rows"), lax.axis_index("cols")
+    entry = jnp.where(everyone >= 0, owner * capacity + rank, 0)
+    places = lax.dynamic_index_in_dim(entry, row * n_cols + col, 0, keepdims=False)
+    places = jnp.minimum(places, n_rows * capacity - 1)
+    group = lambda x: lax.dynamic_index_in_dim(
+        x.reshape(n_rows, n_cols, *x.shape[1:]), col, 1, keepdims=False
+    )
+    picks = (
+        (group(owner) == row)[..., None, :]
+        & group(fresh)[..., None, :]
+        & (group(rank)[..., None, :] == jnp.arange(capacity, dtype=jnp.int32)[:, None])
+    )
+    wanted = jnp.sum(
+        jnp.where(picks, (group(everyone) - row * per_owner)[..., None, :], 0), axis=-1
+    )
+    requests = jnp.swapaxes(wanted, 0, 1).reshape(-1, n_rows * capacity)
+
+    sparse = functools.partial(sparse_program, capacity)
+    if capacity >= min(per_owner, slots):
+        return sparse(places, requests, *args)
+    return lax.cond(
+        most <= capacity,
+        sparse,
+        lambda places, requests, *rest: dense_program(*rest),
+        places, requests, *args,
+    )
+
+
 def solution(mesh):
     return jax.shard_map(
         per_device,

time: 1010 us -> 321 us (0.32)
  waiting for transfers between devices: 838 us -> 0 us
  Pallas kernels: 0 us -> 241 us
  local copies, waits for them, and re-layouts: 67.5 us -> 19.6 us
  other arithmetic: 49.2 us -> 11.9 us
  matrix products: 22 us -> 0 us
  blocking collectives: 12.6 us -> 32.3 us
    reduce_scatter x4 -> x0, waiting for transfers between devices: 595 us -> none  [the longest x2 554 us: per_device(): lax.psum_scatter(local_grad, 'rows', scatter_dimension=1, tiled=True)]
    all_gather x2 -> x0, waiting for transfers between devices: 243 us -> none  [per_device(): lax.all_gather(current.astype(jnp.bfloat16), 'rows', axis=1, tiled=True)]
    pallas_call x0 -> x13, Pallas kernels: none -> 241 us  [the longest x4 182 us: exchange(): pl.pallas_call(functools.partial(exchange_kernel, axis, count), out_shape...]
    reshape x6 -> x0, local copies, waits for them, and re-layouts: 38.7 us -> none  [the longest x2 22.6 us: per_device(): local_grad = jnp.zeros((classes, wide_blocks.shape[1], tile_size), jnp.fl...]
    scatter-add x2 -> x0, other arithmetic: 33 us -> none  [per_device(): local_grad = jnp.zeros((classes, wide_blocks.shape[1], tile_size), jnp.fl...]
    dot_general x6 -> x0, matrix products: 22 us -> none  [the longest x2 9.02 us: per_device(): jnp.einsum('zei,eui->ezu', selected_weights, tile_entries, preferred_elem...]
    all_gather x2 -> x1, blocking collectives: 12.6 us -> 32.3 us  [per_device(): everyone = lax.all_gather(mine, ('rows', 'cols'), axis=0)]
    another operation x2, local copies, waits for them, and re-layouts: 15.7 us -> 0.09 us
  transfers between devices with their start and end apart: 6 -> 0, of which waited for: 6 -> 0; matrix products, arithmetic and copies ran while one was open for 0% -> 0% of each run, Pallas kernels for 0% -> 0%
where the time goes in v1:
time: 321 us; the launch traced here: 320 us
  Pallas kernels  241 us (75%)
  blocking collectives  32.3 us (10%)
  local copies, waits for them, and re-layouts  19.6 us (6%)
  between operations  14.8 us (5%)
  other arithmetic  11.9 us (4%)
    pallas_call x4, Pallas kernels, exchange(): pl.pallas_call(functools.partial(exchange_kernel, axis, count), out_shape...  182 us
    all_gather x1, blocking collectives, per_device(): everyone = lax.all_gather(mine, ('rows', 'cols'), axis=0)  32.3 us
    pallas_call x4, Pallas kernels, slot_call(): pl.pallas_call(functools.partial(kernel, group, size), grid_spec=pltpu.Pr...  26.9 us
    pallas_call x2, Pallas kernels, sparse_program(): pl.pallas_call(functools.partial(classify_kernel, 'cols', n_cols), out_sh...  20.7 us
    cond x24, local copies, waits for them, and re-layouts  13.8 us

profile of v1, /device:TPU:13, one launch (start us, length us, event | category | flops | bytes accessed | tf_op | source)
XLA Modules:
  0.0 320.1 jit_solution(11099850164313086757)
XLA Ops:
  7.9 32.3 %all_gather.16 = s32[32,2,128]{2,1,0:T(2,128)S(1)} all-gather(s32[1,2,128]{2,1,0:T(2,128)S(1)} %compare_select_fusion.10), channel_id=1, replica_groups=mesh['rows'=8,'cols'=4] {'rows','cols'}, dimensions={0}, use_global_device_ids=true | all-gather | bytes 33792 | tf_op jit(solution)/shard_map/all_gather | solution.py:354
  40.3 2.6 and_reduce_fusion
  43.1 4.1 %convert_reduce_fusion = s32[32,2,128]{2,1,0:T(2,128)S(1)} fusion(s32[32,2,128]{2,1,0:T(2,128)S(1)} %all_gather.16, s32[32,2,128]{2,1,0:T(2,128)S(1)} %fusion.61, pred[32,2,128]{2,1,0:T(4,128)(4,1)S(1)} %get-tuple-element.142), kind=kLoop, calls=%fused_computation.118 | loop fusion | flops 6283264 | bytes 106496 | tf_op jit(solution)/shard_map/reduce_sum | solution.py:362
  48.6 1.0 select_reduce_fusion.2
  49.6 263.7 %conditional.1 = (f32[32,16384]{1,0:T(8,128)}, f32[2,256]{1,0:T(2,128)}) conditional(s32[]{:T(128)} %convert_element_type.27, (f32[2]{0:T(128)}, s32[2,1,1,128]{3,2,1,0:T(1,128)}, f32[32,16384]{1,0:T(8,128)}, bf16[2,1,1,128,128,128]{5,4,3,2,1,0:T(8,128)(2,1)}, s32[2,1,1,128]{3,2,1,0:T(1,128)}, /*index=5*/s32[2,1,1]{0,2,1:T(1,128)}, ...), branch_computations={%region_4.17_spmd, %region_15.18_spmd} | conditional | flops 646082816 | bytes 386260672 | solution.py:386
  49.9 1.3 fusion.65
  51.2 2.0 compare_select_fusion
  53.9 1.4 fusion.66
  55.5 1.4 fusion.63
  56.9 2.3 pack.1
  59.2 1.2 copy-done
  60.4 51.8 %exchange.4 = bf16[8,28,32,128]{3,2,1,0:T(8,128)(2,1)} custom-call(bf16[8,28,32,128]{3,2,1,0:T(8,128)(2,1)} %bitcast.144), custom_call_target="tpu_custom_call" | custom-call | tf_op jit(solution)/shard_map/cond/branch_1_fun/exchange/pallas_call | solution.py:150
  112.2 1.5 copy-done.5
  113.7 6.9 %scores.2.part_ref = f32[32,1024]{1,0:T(8,128)S(1)} custom-call(s32[128]{0:T(128)S(1)} %get-tuple-element.153.place_ref, s32[128]{0:T(128)S(1)} %get-tuple-element.151.row_ref, f32[128]{0:T(128)S(1)} %get-tuple-element.149.factor_ref, bf16[224,32,128]{2,1,0:T(8,128)(2,1)S(1)} %bitcast.149, bf16[2,1,1,128,128,128]{5,4,3,2,1,0:T(8,128)(2,1)} %get-tuple-element.88.tiles_ref), custom_call_target="tpu_custom_call" | custom-call | tf_op jit(solution)/shard_map/cond/branch_1_fun/scores/pallas_call | solution.py:253
  121.3 10.6 %classify.2 = (bf16[32,1024]{1,0:T(8,128)(2,1)}, f32[1,1024]{1,0:T(1,128)}) custom-call(f32[32,1024]{1,0:T(8,128)} %copy-done.8, s32[1,1024]{1,0:T(1,128)} %get-tuple-element.145.labels_ref), custom_call_target="tpu_custom_call" | custom-call | tf_op jit(solution)/shard_map/cond/branch_1_fun/classify/pallas_call | solution.py:301
  131.9 0.8 copy-done.11
  132.7 6.6 %grads.2 = bf16[224,32,128]{2,1,0:T(8,128)(2,1)S(1)} custom-call(s32[128]{0:T(128)S(1)} %get-tuple-element.153.place_ref, s32[128]{0:T(128)S(1)} %get-tuple-element.151.row_ref, f32[128]{0:T(128)S(1)} %get-tuple-element.149.factor_ref, bf16[32,1024]{1,0:T(8,128)(2,1)S(1)} %copy-done.11, bf16[2,1,1,128,128,128]{5,4,3,2,1,0:T(8,128)(2,1)} %get-tuple-element.88.tiles_ref), custom_call_target="tpu_custom_call" | custom-call | tf_op jit(solution)/shard_map/cond/branch_1_fun/grads/pallas_call | solution.py:253
  139.3 1.2 copy-done.2
  140.5 42.2 %exchange.5 = bf16[8,28,32,128]{3,2,1,0:T(8,128)(2,1)} custom-call(bf16[8,28,32,128]{3,2,1,0:T(8,128)(2,1)} %bitcast.146), custom_call_target="tpu_custom_call" | custom-call | tf_op jit(solution)/shard_map/cond/branch_1_fun/exchange/pallas_call | solution.py:150
  182.8 1.5 copy-done.1
  184.3 4.7 %apply_pack.1 = (f32[32,16384]{1,0:T(8,128)S(1)}, bf16[224,32,128]{2,1,0:T(8,128)(2,1)S(1)}) custom-call(s32[224]{0:T(256)S(1)} %squeeze.76.next_ref.here_ref, s32[224]{0:T(256)S(1)} %squeeze.75.next_ref.here_ref, f32[1]{0:T(128)} %get-tuple-element.156.rate_ref, f32[32,16384]{1,0:T(8,128)} %get-tuple-element.78.weights_ref, bf16[224,32,128]{2,1,0:T(8,128)(2,1)S(1)} %bitcast.145), custom_call_target="tpu_custom_call" | custom-call | tf_op jit(solution)/shard_map/cond/branch_1_fun/apply_pack/pallas_call | solution.py:327
  189.0 1.2 copy-done.7
  190.2 44.1 %exchange.6 = bf16[8,28,32,128]{3,2,1,0:T(8,128)(2,1)} custom-call(bf16[8,28,32,128]{3,2,1,0:T(8,128)(2,1)} %bitcast.151), custom_call_target="tpu_custom_call" | custom-call | tf_op jit(solution)/shard_map/cond/branch_1_fun/exchange/pallas_call | solution.py:150
  234.3 1.5 copy-done.6
  235.8 6.8 %scores.3.part_ref = f32[32,1024]{1,0:T(8,128)S(1)} custom-call(s32[128]{0:T(128)S(1)} %get-tuple-element.152.place_ref, s32[128]{0:T(128)S(1)} %get-tuple-element.150.row_ref, f32[128]{0:T(128)S(1)} %get-tuple-element.148.factor_ref, bf16[224,32,128]{2,1,0:T(8,128)(2,1)S(1)} %bitcast.150, bf16[2,1,1,128,128,128]{5,4,3,2,1,0:T(8,128)(2,1)} %get-tuple-element.88.tiles_ref), custom_call_target="tpu_custom_call" | custom-call | tf_op jit(solution)/shard_map/cond/branch_1_fun/scores/pallas_call | solution.py:253
  243.3 10.1 %classify.3 = (bf16[32,1024]{1,0:T(8,128)(2,1)}, f32[1,1024]{1,0:T(1,128)}) custom-call(f32[32,1024]{1,0:T(8,128)} %copy-done.9, s32[1,1024]{1,0:T(1,128)} %get-tuple-element.144.labels_ref), custom_call_target="tpu_custom_call" | custom-call | tf_op jit(solution)/shard_map/cond/branch_1_fun/classify/pallas_call | solution.py:301
  254.7 0.8 copy-done.10
  255.6 6.6 %grads.3 = bf16[224,32,128]{2,1,0:T(8,128)(2,1)S(1)} custom-call(s32[128]{0:T(128)S(1)} %get-tuple-element.152.place_ref, s32[128]{0:T(128)S(1)} %get-tuple-element.150.row_ref, f32[128]{0:T(128)S(1)} %get-tuple-element.148.factor_ref, bf16[32,1024]{1,0:T(8,128)(2,1)S(1)} %copy-done.10, bf16[2,1,1,128,128,128]{5,4,3,2,1,0:T(8,128)(2,1)} %get-tuple-element.88.tiles_ref), custom_call_target="tpu_custom_call" | custom-call | tf_op jit(solution)/shard_map/cond/branch_1_fun/grads/pallas_call | solution.py:253
  262.2 1.2 copy-done.3
  263.4 44.1 %exchange.7 = bf16[8,28,32,128]{3,2,1,0:T(8,128)(2,1)} custom-call(bf16[8,28,32,128]{3,2,1,0:T(8,128)(2,1)} %bitcast.147), custom_call_target="tpu_custom_call" | custom-call | tf_op jit(solution)/shard_map/cond/branch_1_fun/exchange/pallas_call | solution.py:150
  307.5 1.5 copy-done.4
  309.0 4.3 %apply.1 = f32[32,16384]{1,0:T(8,128)} custom-call(s32[224]{0:T(256)S(1)} %squeeze.75.next_ref.here_ref, f32[1]{0:T(128)} %get-tuple-element.157.rate_ref, f32[32,16384]{1,0:T(8,128)S(1)} %get-tuple-element.91.weights_ref, bf16[224,32,128]{2,1,0:T(8,128)(2,1)S(1)} %bitcast.148), custom_call_target="tpu_custom_call" | custom-call | tf_op jit(solution)/shard_map/cond/branch_1_fun/apply/pallas_call | solution.py:333
  (35 shorter events, 5.2 us)
Async XLA Ops:
  59.1 1.2 copy-start
  112.2 1.5 copy-start.5
  120.6 0.7 copy-start.8
  131.9 0.8 copy-start.11
  139.3 1.2 copy-start.2
  182.8 1.5 copy-start.1
  189.0 1.2 copy-start.7
  234.3 1.5 copy-start.6
  242.6 0.7 copy-start.9
  254.7 0.8 copy-start.10
  262.2 1.2 copy-start.3
  307.5 1.5 copy-start.4
